TPU v7x, 32 devices: a whole 2x2x4 slice. The times are simulated.
32 devices in a mesh: groups: 2 (over y), space: 4 (over z), clus: 4 (over x, core).
Axes of the slice: x: 2, y: 2, z: 4, core: 2. Of those that a mesh axis runs over, the one named last changes fastest.
Arguments:
- snapshots: bfloat16 [256, 5, 49152], P('groups', None, ('space', 'clus')), parts along dimension 0
- labels: int32 [256], P('groups'), parts along dimension 0, may hold values from 0 to 3, as said below
- start: float32 [256, 16], P('groups'), parts along dimension 0, may hold values from -6 to 6
- successor: int32 [8], P('groups'), parts along dimension 0, may hold values from 0 to 3, as said below
Outputs:
- modes: bfloat16 [8, 16, 5, 49152], P(('groups', 'clus'), None, None, 'space'), parts along dimension 0
- coefficients: float32 [256, 16], P(('groups', 'clus')), parts along dimension 0
- correlations: float32 [8, 16, 16], P(('groups', 'clus')), parts along dimension 0
There are 2 independent parts, one for each index of `groups`. A program takes and returns all parts, laid end to end along the dimension named above; each array names one. Nothing has to cross between parts.
Inputs may be any that keep to these rules, and one draw needn't show every extreme that they name: `labels`: of the 32 snapshots of each aligned block (those of one index of clus), every cluster holds at least 6 and at most 8; in every block some cluster holds exactly 8. Following successor from any cluster visits all 4 clusters once before returning.
All inputs are finite; a program needn't handle non-finite values.
Results may differ from a plain program's by a relative error of at most 0.0045.
Values may be sent and summed in bfloat16 or wider, within the bound.
No kernel may reach another device: no remote copies, remote signals or barrier semaphores. Data moves between devices by JAX's collectives and lax.ppermute only.
A program may use at most 64 MiB of HBM per device.

v0:
```python
import jax
import jax.numpy as jnp
from jax import lax
from jax.sharding import PartitionSpec as P

ITERS = 2


def subspace(gram, member, start):
    basis = member[:, :, None] * start[None, :, :]
    for step in range(ITERS):
        image = (
            member[:, :, None]
            * jnp.einsum("st,ktm->ksm", gram, basis, precision=lax.Precision.HIGHEST)
            + basis
        )
        inner = jnp.einsum("ksm,ksn->kmn", image, image, precision=lax.Precision.HIGHEST)
        lower = jnp.linalg.cholesky(inner)
        basis = lax.linalg.triangular_solve(
            lower, image, left_side=False, lower=True, transpose_a=True
        )
    return basis


def local(snapshots, labels, start, successor):
    count, variables, cells = snapshots.shape
    clusters = lax.axis_size("clus")
    owner = lax.axis_index("clus")
    total_rows = variables * cells * lax.axis_size("space") * clusters
    flat = snapshots.reshape(count, variables * cells)
    partial_value = lax.dot_general(
        flat, flat, (((1,), (1,)), ((), ())), preferred_element_type=jnp.float32
    )
    gram = lax.psum(partial_value, ("space", "clus")) / total_rows
    cluster_ids = jnp.arange(clusters, dtype=jnp.int32)
    member = (labels[None, :] == cluster_ids[:, None]).astype(jnp.float32)
    basis = subspace(gram, member, start)
    picked = jnp.einsum("ks,ksm->sm", member, basis, precision=lax.Precision.HIGHEST)
    snap_dev = count // clusters
    coefficients = lax.dynamic_slice_in_dim(picked, owner * snap_dev, snap_dev, 0)
    rounded = basis.astype(jnp.bfloat16)
    mode_count = rounded.shape[2]
    modes_full = None
    left = jnp.transpose(rounded, (0, 2, 1)).reshape(clusters * mode_count, count)
    modes_full = jnp.dot(left, flat, preferred_element_type=jnp.float32)
    packed = modes_full.astype(jnp.bfloat16).reshape(clusters, mode_count, variables, cells)
    modes_out = lax.all_to_all(packed, "clus", split_axis=0, concat_axis=3, tiled=True)
    select = (successor[:, None] == cluster_ids[None, :]).astype(jnp.float32)
    wide = rounded.astype(jnp.float32)
    partner = jnp.einsum("ab,bsn->asn", select, wide, precision=lax.Precision.HIGHEST)
    image = jnp.einsum("st,atn->asn", gram, partner, precision=lax.Precision.HIGHEST)
    correlations = jnp.einsum("asm,asn->amn", wide, image, precision=lax.Precision.HIGHEST)
    own_correlation = lax.dynamic_slice_in_dim(correlations, owner, 1, 0)
    return (modes_out, coefficients, own_correlation)


def solution(mesh):
    in_specs = (P("groups", None, ("space", "clus")), P("groups"), P("groups", None), P("groups"))
    out_specs = (
        P(("groups", "clus"), None, None, "space"),
        P(("groups", "clus"), None),
        P(("groups", "clus"), None, None),
    )
    return jax.shard_map(local, mesh=mesh, in_specs=in_specs, out_specs=out_specs, check_vma=False)
```

profile of v0, /device:TPU:8, one launch (start us, length us, event | category | flops | bytes accessed | tf_op | source)
XLA Modules:
  0.0 174.2 jit_solution(173776694287602055)
XLA Ops:
  7.2 0.0 all-reduce.2.cloned.1.call-start
  7.2 5.1 %convolution_bitcast_fusion = f32[128,128]{1,0:T(8,128)} fusion(bf16[128,5,3072]{2,0,1:T(8,128)(2,1)} %param.7), kind=kOutput, calls=%fused_computation.1 | convolution fusion | flops 503316480 | bytes 3997696 | tf_op jit(solution)/shard_map/dot_general | solution.py:31
  12.4 0.0 all-reduce.2.cloned.1.call-update
  12.4 6.3 %copy.38 = bf16[128,5,3072]{0,2,1:T(8,128)(2,1)} copy(bf16[128,5,3072]{2,0,1:T(8,128)(2,1)} %param.7) | data formatting | bytes 7864320 | tf_op args[0]
  18.7 82.0 %all-reduce.2.cloned.1.call-done = f32[128,128]{1,0:T(8,128)} async-done(((f32[128,128]{1,0:T(8,128)}), f32[128,128]{1,0:T(8,128)}) %all-reduce.2.cloned.1.call-update) | async-done | bytes 65552 | tf_op jit(solution)/shard_map/psum | solution.py:34
  100.7 1.1 fusion.3
  101.8 0.2 fusion.35
  102.0 0.1 copy.34
  102.1 5.9 %custom-call.8 = f32[4,16,16]{2,1,0:T(8,128)S(1)} custom-call(f32[4,16,16]{2,1,0:T(8,128)S(1)} %fusion.16), custom_call_target="Cholesky" | custom-call | tf_op jit(solution)/shard_map/jit(cholesky)/cholesky | solution.py:18
  108.0 0.1 compare_reduce_fusion.1
  108.1 0.1 select_bitcast_fusion.1
  108.2 4.9 %custom-call.9 = f32[4,1,16,16]{2,3,1,0:T(8,128)S(1)} custom-call(f32[4,1,16,16]{3,2,1,0:T(8,128)S(1)} %select_bitcast_fusion.1), custom_call_target="InvertDiagBlocksLowerTriangular" | custom-call | tf_op jit(solution)/shard_map/triangular_solve/custom-call.0 | solution.py:19
  113.1 0.3 convolution_bitcast_fusion.1
  113.4 1.1 fusion.1
  114.5 0.2 fusion.36
  114.6 0.1 copy.36
  114.7 5.9 %custom-call.10 = f32[4,16,16]{2,1,0:T(8,128)S(1)} custom-call(f32[4,16,16]{2,1,0:T(8,128)S(1)} %fusion.14), custom_call_target="Cholesky" | custom-call | tf_op jit(solution)/shard_map/jit(cholesky)/cholesky | solution.py:18
  120.6 0.1 compare_reduce_fusion
  120.7 0.1 select_bitcast_fusion
  120.8 4.9 %custom-call.11 = f32[4,1,16,16]{2,3,1,0:T(8,128)S(1)} custom-call(f32[4,1,16,16]{3,2,1,0:T(8,128)S(1)} %select_bitcast_fusion), custom_call_target="InvertDiagBlocksLowerTriangular" | custom-call | tf_op jit(solution)/shard_map/triangular_solve/custom-call.0 | solution.py:19
  125.7 0.3 bitcast_convert_fusion
  126.0 4.9 %convolution_convert_fusion = bf16[64,15360]{1,0:T(8,128)(2,1)} fusion(bf16[64,128]{1,0:T(8,128)(2,1)S(1)} %bitcast.78, bf16[128,15360]{0,1:T(8,128)(2,1)} %bitcast.75), kind=kOutput, calls=%fused_computation | convolution fusion | flops 252641280 | bytes 5914624 | tf_op jit(solution)/shard_map/dot_general | solution.py:45
  130.9 4.6 %reshape.50 = bf16[4,16,5,3072]{3,2,1,0:T(8,128)(2,1)S(1)} reshape(bf16[64,15360]{1,0:T(8,128)(2,1)} %convolution_convert_fusion) | data formatting | bytes 3932160 | tf_op jit(solution)/shard_map/reshape | solution.py:46
  135.5 2.6 %copy.39 = bf16[4,16,5,3072]{3,1,2,0:T(8,128)(2,1)} copy(bf16[4,16,5,3072]{3,2,1,0:T(8,128)(2,1)S(1)} %reshape.50) | data formatting | bytes 3932160 | tf_op jit(solution)/shard_map/reshape | solution.py:46
  138.1 3.6 %all-to-all-start = ((bf16[4,16,5,3072]{3,1,2,0:T(8,128)(2,1)}), bf16[4,16,5,3072]{3,1,2,0:T(8,128)(2,1)S(1)}, u32[]{:S(2)}, u32[]{:S(2)}) async-start(bf16[4,16,5,3072]{3,1,2,0:T(8,128)(2,1)} %copy.39), calls=%async_computation | async-start | bytes 3932160 | tf_op jit(solution)/shard_map/all_to_all | solution.py:47
  141.7 0.7 constant_dynamic-slice_fusion.1
  142.4 0.2 fusion.22
  142.6 0.2 fusion.4
  142.8 0.1 fusion.37
  143.0 0.6 constant_dynamic-slice_fusion
  143.6 22.4 %all-to-all-done = bf16[4,16,5,3072]{3,1,2,0:T(8,128)(2,1)S(1)} async-done(((bf16[4,16,5,3072]{3,1,2,0:T(8,128)(2,1)}), bf16[4,16,5,3072]{3,1,2,0:T(8,128)(2,1)S(1)}, u32[]{:S(2)}, u32[]{:S(2)}) %all-to-all-start) | async-done | bytes 1966112 | tf_op jit(solution)/shard_map/all_to_all | solution.py:47
  165.9 1.4 copy.52
  (16 shorter events, 0.1 us)
Async XLA Ops:
  7.2 5.2 %copy-start.2 = (s32[128]{0:T(128)S(1)}, s32[128]{0:T(128)}, u32[]{:S(2)}) copy-start(s32[128]{0:T(128)} %param.8) | copy-start | bytes 1540
  7.2 93.5 %all-reduce.2.cloned.1.call-start = ((), (), s32[]{:S(2)}) async-start(), calls=%async_computation.1 | async-start | bytes 131072 | tf_op jit(solution)/shard_map/psum | solution.py:34
  12.4 88.3 %copy-start.1 = (f32[128,16]{0,1:T(8,128)S(1)}, f32[128,16]{0,1:T(8,128)}, u32[]{:S(2)}) copy-start(f32[128,16]{0,1:T(8,128)} %param.9) | copy-start | bytes 24580
  135.5 6.9 %copy-start.3 = (s32[4]{0:T(128)S(1)}, s32[4]{0:T(128)}, u32[]{:S(2)}) copy-start(s32[4]{0:T(128)} %param.10) | copy-start | bytes 52
  135.5 7.1 %copy-start = (f32[128,128]{1,0:T(8,128)S(1)}, f32[128,128]{1,0:T(8,128)}, u32[]{:S(2)}) copy-start(f32[128,128]{1,0:T(8,128)} %all-reduce.2.cloned.1.call-done) | copy-start | bytes 196612
  138.1 27.9 %all-to-all-start = ((bf16[4,16,5,3072]{3,1,2,0:T(8,128)(2,1)}), bf16[4,16,5,3072]{3,1,2,0:T(8,128)(2,1)S(1)}, u32[]{:S(2)}, u32[]{:S(2)}) async-start(bf16[4,16,5,3072]{3,1,2,0:T(8,128)(2,1)} %copy.39), calls=%async_computation | async-start | bytes 3932160 | tf_op jit(solution)/shard_map/all_to_all | solution.py:47
Sparse Core Ops, SparseCore 0:
  12.5 88.1 all-reduce.1
where the time goes:
time: 175 us; the launch traced here: 174 us
  waiting for transfers between devices  104 us (59%)
  other arithmetic  22.1 us (13%)
  local copies, waits for them, and re-layouts  16.3 us (9%)
  between operations  14.2 us (8%)
  matrix products  13.6 us (8%)
  starting transfers between devices  3.64 us (2%)
    psum x1, waiting for transfers between devices, local(): gram = lax.psum(partial_value, ('space', 'clus')) / total_rows  82 us
    all_to_all x1, waiting for transfers between devices, local(): lax.all_to_all(packed, 'clus', split_axis=0, concat_axis=3, tiled=True)  22.4 us
    another operation x7, other arithmetic, subspace(): lower = jnp.linalg.cholesky(inner)  12 us
    another operation x5, other arithmetic, subspace(): lax.linalg.triangular_solve(lower, image, left_side=False, lower=True, tr...  9.99 us
    reshape x2, local copies, waits for them, and re-layouts, local(): modes_full.astype(jnp.bfloat16)  7.12 us
    unnamed x9, local copies, waits for them, and re-layouts  6.29 us
    dot_general x1, matrix products, local(): lax.dot_general(flat, flat, (((1,), (1,)), ((), ())), preferred_element_t...  5.13 us
    dot_general x1, matrix products, local(): modes_full = jnp.dot(left, flat, preferred_element_type=jnp.float32)  4.86 us
  transfers between devices with their start and end apart: 2, of which 2 were waited for; matrix products, arithmetic and copies ran while one was open for 5% of the time, Pallas kernels for 0%

commit v1 on v0

--- a/solution.py
+++ b/solution.py
@@ -31,7 +31,7 @@
     partial_value = lax.dot_general(
         flat, flat, (((1,), (1,)), ((), ())), preferred_element_type=jnp.float32
     )
-    gram = lax.psum(partial_value, ("space", "clus")) / total_rows
+    gram = lax.psum(lax.psum(partial_value, "clus"), "space") / total_rows
     cluster_ids = jnp.arange(clusters, dtype=jnp.int32)
     member = (labels[None, :] == cluster_ids[:, None]).astype(jnp.float32)
     basis = subspace(gram, member, start)

time: 175 us -> 157 us (0.90)
  waiting for transfers between devices: 104 us -> 84.7 us
    psum x1 -> x2, waiting for transfers between devices: 82 us -> 62.3 us  [local(): gram = lax.psum(lax.psum(partial_value, 'clus'), 'space') / total_rows]
  transfers between devices with their start and end apart: 2 -> 3, of which waited for: 2 -> 3; matrix products, arithmetic and copies ran while one was open for 5% -> 5% of each run, Pallas kernels for 0% -> 0%
where the time goes in v1:
time: 157 us; the launch traced here: 155 us
  waiting for transfers between devices  84.7 us (54%)
  other arithmetic  22.1 us (14%)
  local copies, waits for them, and re-layouts  16.3 us (10%)
  between operations  14.2 us (9%)
  matrix products  13.7 us (9%)
  starting transfers between devices  3.68 us (2%)
    psum x2, waiting for transfers between devices, local(): gram = lax.psum(lax.psum(partial_value, 'clus'), 'space') / total_rows  62.3 us
    all_to_all x1, waiting for transfers between devices, local(): lax.all_to_all(packed, 'clus', split_axis=0, concat_axis=3, tiled=True)  22.4 us
    another operation x7, other arithmetic, subspace(): lower = jnp.linalg.cholesky(inner)  12 us
    another operation x5, other arithmetic, subspace(): lax.linalg.triangular_solve(lower, image, left_side=False, lower=True, tr...  9.99 us
    reshape x2, local copies, waits for them, and re-layouts, local(): modes_full.astype(jnp.bfloat16)  7.12 us
    unnamed x9, local copies, waits for them, and re-layouts  6.29 us
    dot_general x1, matrix products, local(): lax.dot_general(flat, flat, (((1,), (1,)), ((), ())), preferred_element_t...  5.13 us
    dot_general x1, matrix products, local(): modes_full = jnp.dot(left, flat, preferred_element_type=jnp.float32)  4.86 us
  transfers between devices with their start and end apart: 3, of which 3 were waited for; matrix products, arithmetic and copies ran while one was open for 5% of the time, Pallas kernels for 0%

profile of v1, /device:TPU:8, one launch (start us, length us, event | category | flops | bytes accessed | tf_op | source)
XLA Modules:
  0.0 154.6 jit_solution(17906495576228358992)
XLA Ops:
  7.2 5.1 %convolution_bitcast_fusion = f32[128,128]{1,0:T(8,128)} fusion(bf16[128,5,3072]{2,0,1:T(8,128)(2,1)} %param.7), kind=kOutput, calls=%fused_computation.1 | convolution fusion | flops 503316480 | bytes 3997696 | tf_op jit(solution)/shard_map/dot_general | solution.py:31
  12.4 0.0 all-reduce.5.cloned.1.call-start
  12.5 6.3 %copy.38 = bf16[128,5,3072]{0,2,1:T(8,128)(2,1)} copy(bf16[128,5,3072]{2,0,1:T(8,128)(2,1)} %param.7) | data formatting | bytes 7864320 | tf_op args[0]
  18.7 26.0 %all-reduce.3.cloned.1.call-done = f32[128,128]{1,0:T(8,128)} async-done(((f32[128,128]{1,0:T(8,128)}), f32[128,128]{1,0:T(8,128)}) %all-reduce.3.cloned.1.call-update) | async-done | bytes 65552 | tf_op jit(solution)/shard_map/psum | solution.py:34
  44.8 36.3 %all-reduce.5.cloned.1.call-done = f32[128,128]{1,0:T(8,128)} async-done(((f32[128,128]{1,0:T(8,128)}), f32[128,128]{1,0:T(8,128)}) %all-reduce.5.cloned.1.call-update) | async-done | bytes 65552 | tf_op jit(solution)/shard_map/psum | solution.py:34
  81.1 1.1 fusion.3
  82.2 0.2 fusion.35
  82.4 0.1 copy.34
  82.5 5.9 %custom-call.8 = f32[4,16,16]{2,1,0:T(8,128)S(1)} custom-call(f32[4,16,16]{2,1,0:T(8,128)S(1)} %fusion.16), custom_call_target="Cholesky" | custom-call | tf_op jit(solution)/shard_map/jit(cholesky)/cholesky | solution.py:18
  88.4 0.1 compare_reduce_fusion.1
  88.5 0.1 select_bitcast_fusion.1
  88.5 4.9 %custom-call.9 = f32[4,1,16,16]{2,3,1,0:T(8,128)S(1)} custom-call(f32[4,1,16,16]{3,2,1,0:T(8,128)S(1)} %select_bitcast_fusion.1), custom_call_target="InvertDiagBlocksLowerTriangular" | custom-call | tf_op jit(solution)/shard_map/triangular_solve/custom-call.0 | solution.py:19
  93.5 0.3 convolution_bitcast_fusion.1
  93.8 1.1 fusion.1
  94.9 0.2 fusion.36
  95.0 0.1 copy.36
  95.1 5.9 %custom-call.10 = f32[4,16,16]{2,1,0:T(8,128)S(1)} custom-call(f32[4,16,16]{2,1,0:T(8,128)S(1)} %fusion.14), custom_call_target="Cholesky" | custom-call | tf_op jit(solution)/shard_map/jit(cholesky)/cholesky | solution.py:18
  101.0 0.1 compare_reduce_fusion
  101.1 0.1 select_bitcast_fusion
  101.2 4.9 %custom-call.11 = f32[4,1,16,16]{2,3,1,0:T(8,128)S(1)} custom-call(f32[4,1,16,16]{3,2,1,0:T(8,128)S(1)} %select_bitcast_fusion), custom_call_target="InvertDiagBlocksLowerTriangular" | custom-call | tf_op jit(solution)/shard_map/triangular_solve/custom-call.0 | solution.py:19
  106.1 0.3 bitcast_convert_fusion
  106.4 4.9 %convolution_convert_fusion = bf16[64,15360]{1,0:T(8,128)(2,1)} fusion(bf16[64,128]{1,0:T(8,128)(2,1)S(1)} %bitcast.78, bf16[128,15360]{0,1:T(8,128)(2,1)} %bitcast.75), kind=kOutput, calls=%fused_computation | convolution fusion | flops 252641280 | bytes 5914624 | tf_op jit(solution)/shard_map/dot_general | solution.py:45
  111.3 4.6 %reshape.50 = bf16[4,16,5,3072]{3,2,1,0:T(8,128)(2,1)S(1)} reshape(bf16[64,15360]{1,0:T(8,128)(2,1)} %convolution_convert_fusion) | data formatting | bytes 3932160 | tf_op jit(solution)/shard_map/reshape | solution.py:46
  115.9 2.6 %copy.39 = bf16[4,16,5,3072]{3,1,2,0:T(8,128)(2,1)} copy(bf16[4,16,5,3072]{3,2,1,0:T(8,128)(2,1)S(1)} %reshape.50) | data formatting | bytes 3932160 | tf_op jit(solution)/shard_map/reshape | solution.py:46
  118.5 3.6 %all-to-all-start = ((bf16[4,16,5,3072]{3,1,2,0:T(8,128)(2,1)}), bf16[4,16,5,3072]{3,1,2,0:T(8,128)(2,1)S(1)}, u32[]{:S(2)}, u32[]{:S(2)}) async-start(bf16[4,16,5,3072]{3,1,2,0:T(8,128)(2,1)} %copy.39), calls=%async_computation | async-start | bytes 3932160 | tf_op jit(solution)/shard_map/all_to_all | solution.py:47
  122.1 0.7 constant_dynamic-slice_fusion.1
  122.8 0.2 fusion.22
  123.0 0.2 fusion.4
  123.2 0.1 fusion.37
  123.3 0.6 constant_dynamic-slice_fusion
  124.0 22.4 %all-to-all-done = bf16[4,16,5,3072]{3,1,2,0:T(8,128)(2,1)S(1)} async-done(((bf16[4,16,5,3072]{3,1,2,0:T(8,128)(2,1)}), bf16[4,16,5,3072]{3,1,2,0:T(8,128)(2,1)S(1)}, u32[]{:S(2)}, u32[]{:S(2)}) %all-to-all-start) | async-done | bytes 1966112 | tf_op jit(solution)/shard_map/all_to_all | solution.py:47
  146.3 1.4 copy.52
  (19 shorter events, 0.2 us)
Async XLA Ops:
  7.2 5.3 %copy-start.2 = (s32[128]{0:T(128)S(1)}, s32[128]{0:T(128)}, u32[]{:S(2)}) copy-start(s32[128]{0:T(128)} %param.8) | copy-start | bytes 1540
  7.2 37.5 %all-reduce.3.cloned.1.call-start = ((), (), s32[]{:S(2)}) async-start(), calls=%async_computation.1 | async-start | bytes 131072 | tf_op jit(solution)/shard_map/psum | solution.py:34
  12.4 68.7 %all-reduce.5.cloned.1.call-start = ((), (), s32[]{:S(2)}) async-start(), calls=%async_computation.2 | async-start | bytes 131072 | tf_op jit(solution)/shard_map/psum | solution.py:34
  12.5 68.6 %copy-start.1 = (f32[128,16]{0,1:T(8,128)S(1)}, f32[128,16]{0,1:T(8,128)}, u32[]{:S(2)}) copy-start(f32[128,16]{0,1:T(8,128)} %param.9) | copy-start | bytes 24580
  115.9 6.9 %copy-start.3 = (s32[4]{0:T(128)S(1)}, s32[4]{0:T(128)}, u32[]{:S(2)}) copy-start(s32[4]{0:T(128)} %param.10) | copy-start | bytes 52
  115.9 7.1 %copy-start = (f32[128,128]{1,0:T(8,128)S(1)}, f32[128,128]{1,0:T(8,128)}, u32[]{:S(2)}) copy-start(f32[128,128]{1,0:T(8,128)} %all-reduce.5.cloned.1.call-done) | copy-start | bytes 196612
  118.5 27.9 %all-to-all-start = ((bf16[4,16,5,3072]{3,1,2,0:T(8,128)(2,1)}), bf16[4,16,5,3072]{3,1,2,0:T(8,128)(2,1)S(1)}, u32[]{:S(2)}, u32[]{:S(2)}) async-start(bf16[4,16,5,3072]{3,1,2,0:T(8,128)(2,1)} %copy.39), calls=%async_computation | async-start | bytes 3932160 | tf_op jit(solution)/shard_map/all_to_all | solution.py:47
Sparse Core Ops, SparseCore 0:
  12.5 32.1 all-reduce.2
  47.1 33.9 all-reduce.4
